TPU v7x, 256 devices: a whole 4x4x8 slice. The times are simulated.
256 devices in a mesh: row: 16 (over y, z_hi), col: 16 (over x, z_lo, core).
Axes of the slice: x: 4, y: 4, z: 8 (z_hi: 4, z_lo: 2; z = z_hi * 2 + z_lo), core: 2. Of those that a mesh axis runs over, the one named last changes fastest.
Arguments:
- image: bfloat16 [512, 512, 192], P('row', 'col'), may hold values from -6 to 6
- conv_weight: bfloat16 [3, 3, 192, 384], replicated, may hold values from -0.15625 to 0.15625
- conv_bias: float32 [384], replicated, may hold values from -3 to 3
- merge_gain: float32 [384], replicated, may hold values from 0.25 to 1.75
- merge_shift: float32 [384], replicated, may hold values from -3 to 3
- norm_gain: float32 [384], replicated, may hold values from 0.25 to 1.75
- norm_shift: float32 [384], replicated, may hold values from -3 to 3
- qkv_weight: bfloat16 [384, 1152], replicated, may hold values from -4 to 4
- proj_weight: bfloat16 [384, 384], replicated, may hold values from -0.3125 to 0.3125
- proj_bias: float32 [384], replicated, may hold values from -3 to 3
Outputs:
- block_out: bfloat16 [256, 256, 384], P('row', 'col')
All inputs are finite; a program needn't handle non-finite values.
Results may differ from a plain program's by a relative error of at most 0.02.
The roundings to bfloat16 on the way count: a program that leaves them out, or rounds other values in their place, can miss the bound.
Values may be sent and summed in bfloat16 or wider, within the bound.
A program may use at most 128 MiB of HBM per device.

v0:
```python
import math

import jax
import jax.numpy as jnp
from jax import lax
from jax.sharding import PartitionSpec as P

HEADS = 16
SPLIT = 8


def shifted(value, axis, steps):
    count = lax.axis_size(axis)
    initial, last = (max(0, -steps), min(count, count - steps))
    return lax.ppermute(value, axis, [(source, source + steps) for source in range(initial, last)])


def layer_norm(values, gain, shift):
    center = values - jnp.mean(values, -1, keepdims=True)
    spread = jnp.mean(center * center, -1, keepdims=True)
    return center * lax.rsqrt(spread + 1e-05) * gain + shift


def start_state(queries):
    count, length, depth = queries.shape
    return (
        jnp.full((count, length), -1e30, jnp.float32),
        jnp.zeros((count, length), jnp.float32),
        jnp.zeros((count, depth, length), jnp.float32),
    )


def online_step(carry, queries, key_rows, value_rows):
    highest, totals, summed = carry
    scores = jnp.einsum("nqd,nkd->nqk", queries, key_rows, preferred_element_type=jnp.float32)
    scores = scores / math.sqrt(queries.shape[-1])
    raised = jnp.maximum(highest, jnp.max(scores, -1))
    weights = jnp.exp(scores - raised[..., None])
    totals = jnp.sum(weights, -1)
    summed = jnp.einsum(
        "nqk,nkd->ndq", weights.astype(jnp.bfloat16), value_rows, preferred_element_type=jnp.float32
    )
    return (raised, totals, summed)


def on_device(
    image,
    conv_weight,
    conv_bias,
    merge_gain,
    merge_shift,
    norm_gain,
    norm_shift,
    qkv_weight,
    proj_weight,
    proj_bias,
):
    in_rows, in_cols, channels = image.shape
    tile_rows = in_rows // 2
    tile_cols = in_cols // 2
    width = conv_weight.shape[3]
    heads_half = HEADS // 2
    depth = width // HEADS
    stripe = SPLIT
    upper = shifted(image[-1:], "row", 1)
    taller = jnp.concatenate([upper, image], 0)
    beside = shifted(taller[:, -1:], "col", 1)
    padded = jnp.concatenate([beside, taller], 1)
    merged = jnp.zeros((tile_rows * tile_cols, width), jnp.float32)
    for tap_row in range(3):
        for tap_col in range(3):
            window = padded[
                tap_row : tap_row + 2 * tile_rows : 2, tap_col : tap_col + 2 * tile_cols : 2
            ]
            merged = merged + jnp.dot(
                window.reshape(tile_rows * tile_cols, channels),
                conv_weight[tap_row, tap_col],
                preferred_element_type=jnp.float32,
            )
    tokens = layer_norm(merged + conv_bias, merge_gain, merge_shift).astype(jnp.bfloat16)
    normed = layer_norm(tokens.astype(jnp.float32), norm_gain, norm_shift).astype(jnp.bfloat16)
    projected = jnp.dot(normed, qkv_weight, preferred_element_type=jnp.float32).astype(jnp.bfloat16)
    projected = projected.reshape(tile_rows, tile_cols, 3, 2, heads_half, depth)
    row_count = tile_rows // stripe
    col_count = tile_cols // stripe
    row_part = projected[:, :, :, 0].reshape(row_count, stripe, tile_cols, 3, heads_half, depth)
    col_part = projected[:, :, :, 1].reshape(tile_rows, col_count, stripe, 3, heads_half, depth)
    row_query = (
        row_part[:, :, :, 0]
        .transpose(0, 3, 1, 2, 4)
        .reshape(row_count * heads_half, stripe * tile_cols, depth)
    )
    row_pairs = row_part[:, :, :, 1:].transpose(3, 0, 4, 1, 2, 5)
    piece = lax.all_gather(row_pairs, "col", axis=4, tiled=True)
    span = piece.shape[4]
    key_rows = piece[0].reshape(row_count * heads_half, stripe * span, depth)
    value_rows = piece[1].reshape(row_count * heads_half, stripe * span, depth)
    row_state = online_step(start_state(row_query), row_query, key_rows, value_rows)
    row_out = (row_state[2] / row_state[1][:, None, :]).astype(jnp.bfloat16)
    row_out = row_out.reshape(row_count, heads_half, depth, stripe, tile_cols).transpose(
        0, 3, 4, 1, 2
    )
    row_out = row_out.reshape(tile_rows, tile_cols, heads_half, depth)
    col_query = (
        col_part[:, :, :, 0]
        .transpose(1, 3, 0, 2, 4)
        .reshape(col_count * heads_half, tile_rows * stripe, depth)
    )
    col_pairs = col_part[:, :, :, 1:].transpose(3, 1, 4, 0, 2, 5)
    piece = lax.all_gather(col_pairs, "row", axis=3, tiled=True)
    span = piece.shape[3]
    key_rows = piece[0].reshape(col_count * heads_half, span * stripe, depth)
    value_rows = piece[1].reshape(col_count * heads_half, span * stripe, depth)
    col_state = online_step(start_state(col_query), col_query, key_rows, value_rows)
    col_out = (col_state[2] / col_state[1][:, None, :]).astype(jnp.bfloat16)
    col_out = col_out.reshape(col_count, heads_half, depth, tile_rows, stripe).transpose(
        3, 0, 4, 1, 2
    )
    col_out = col_out.reshape(tile_rows, tile_cols, heads_half, depth)
    attention = jnp.concatenate([row_out, col_out], 2).reshape(tile_rows * tile_cols, width)
    output = (
        tokens.astype(jnp.float32)
        + jnp.dot(attention, proj_weight, preferred_element_type=jnp.float32)
        + proj_bias
    )
    return output.astype(jnp.bfloat16).reshape(tile_rows, tile_cols, width)


def solution(mesh):
    return jax.shard_map(
        on_device,
        mesh=mesh,
        in_specs=(P("row", "col", None), P(), P(), P(), P(), P(), P(), P(), P(), P()),
        out_specs=P("row", "col", None),
        check_vma=False,
    )
```

profile of v0, /device:TPU:32, one launch (start us, length us, event | category | flops | bytes accessed | tf_op | source)
XLA Modules:
  0.0 437.7 jit_solution(101655848057707000)
XLA Ops:
  7.4 5.2 %collective-permute-start = (bf16[1,32,192]{2,1,0:T(8,128)(2,1)S(1)}, bf16[1,32,192]{2,1,0:T(8,128)(2,1)S(1)}, u32[]{:S(2)}, u32[]{:S(2)}) collective-permute-start(bf16[1,32,192]{2,1,0:T(8,128)(2,1)S(1)} %slice.90), channel_id=1, source_target_pairs={{0,16},{16,32},{32,48},{48,64},{64,80},{80,96},{96,112},{112,128},... | collective-permute-start | bytes 36872 | tf_op jit(solution)/shard_map/ppermute | solution.py:15
  12.6 6.3 %slice.100 = bf16[16,16,192]{2,1,0:T(8,128)(2,1)S(1)} slice(bf16[32,32,192]{2,1,0:T(8,128)(2,1)} %param.10), slice={[0:32:2], [0:32:2], [0:192:1]} | slice | bytes 196608 | tf_op jit(solution)/shard_map/slice | solution.py:72
  18.8 6.3 %slice.102 = bf16[16,16,192]{2,1,0:T(8,128)(2,1)S(1)} slice(bf16[32,32,192]{2,1,0:T(8,128)(2,1)} %param.10), slice={[0:32:2], [1:32:2], [0:192:1]} | slice | bytes 196608 | tf_op jit(solution)/shard_map/slice | solution.py:72
  25.1 6.3 %slice.106 = bf16[16,16,192]{2,1,0:T(8,128)(2,1)S(1)} slice(bf16[32,32,192]{2,1,0:T(8,128)(2,1)} %param.10), slice={[1:32:2], [0:32:2], [0:192:1]} | slice | bytes 196608 | tf_op jit(solution)/shard_map/slice | solution.py:72
  31.4 6.3 %slice.108 = bf16[16,16,192]{2,1,0:T(8,128)(2,1)S(1)} slice(bf16[32,32,192]{2,1,0:T(8,128)(2,1)} %param.10), slice={[1:32:2], [1:32:2], [0:192:1]} | slice | bytes 196608 | tf_op jit(solution)/shard_map/slice | solution.py:72
  39.3 1.9 collective-permute-start.1
  57.4 5.4 %reshape.101 = bf16[16,16,3,2,8,24]{5,4,3,2,1,0:T(8,128)(2,1)} reshape(bf16[256,1152]{1,0:T(8,128)(2,1)S(1)} %convolution_convert_fusion) | data formatting | bytes 1179648 | tf_op jit(solution)/shard_map/reshape | solution.py:83
  62.8 2.4 fusion.59
  72.3 91.2 %all-gather.3.cloned.1.call-done = bf16[2,2,8,8,256,24]{5,2,0,4,3,1:T(8,128)(2,1)} async-done(((bf16[2,2,8,8,16,24]{5,2,0,4,3,1:T(8,128)(2,1)}), bf16[2,2,8,8,256,24]{5,2,0,4,3,1:T(8,128)(2,1)}) %all-gather.3.cloned.1.call-update) | async-done | bytes 3145744 | tf_op jit(solution)/shard_map/all_gather | solution.py:94
  163.5 11.4 %fusion.57 = (bf16[1,2,8,8,256,24]{5,2,0,4,3,1:T(8,128)(2,1)}, bf16[1,2,8,8,256,24]{5,2,0,4,3,1:T(8,128)(2,1)}) fusion(bf16[2,2,8,8,256,24]{5,2,0,4,3,1:T(8,128)(2,1)} %all-gather.3.cloned.1.call-done), kind=kLoop, calls=%fused_computation.78 | loop fusion | bytes 6291456 | tf_op jit(solution)/shard_map/slice | solution.py:96
  174.9 7.9 %copy.38 = bf16[1,2,8,8,256,24]{4,3,5,2,1,0:T(8,128)(2,1)S(1)} copy(bf16[1,2,8,8,256,24]{5,2,0,4,3,1:T(8,128)(2,1)} %get-tuple-element.7) | data formatting | bytes 3145728 | tf_op jit(solution)/shard_map/slice | solution.py:96
  182.8 2.1 reshape_squeeze.20
  184.9 7.6 %copy.36 = bf16[1,2,8,8,256,24]{4,3,5,2,1,0:T(8,128)(2,1)S(1)} copy(bf16[1,2,8,8,256,24]{5,2,0,4,3,1:T(8,128)(2,1)} %get-tuple-element.8) | data formatting | bytes 3145728 | tf_op jit(solution)/shard_map/slice | solution.py:97
  192.6 2.1 reshape_squeeze.19
  194.7 3.9 multiply_reduce_fusion.1
  198.5 3.3 fusion
  201.8 4.2 fusion.22
  207.2 160.3 %all-gather.5.cloned.1.call-done = bf16[2,2,8,256,8,24]{5,4,2,1,0,3:T(8,128)(2,1)} async-done(((bf16[2,2,8,16,8,24]{5,4,2,1,0,3:T(8,128)(2,1)}), bf16[2,2,8,256,8,24]{5,4,2,1,0,3:T(8,128)(2,1)}) %all-gather.5.cloned.1.call-update) | async-done | bytes 3145744 | tf_op jit(solution)/shard_map/all_gather | solution.py:110
  367.5 14.9 %fusion.58 = (bf16[1,2,8,256,8,24]{5,4,2,1,0,3:T(8,128)(2,1)}, bf16[1,2,8,256,8,24]{5,4,2,1,0,3:T(8,128)(2,1)}) fusion(bf16[2,2,8,256,8,24]{5,4,2,1,0,3:T(8,128)(2,1)} %all-gather.5.cloned.1.call-done), kind=kLoop, calls=%fused_computation.79 | loop fusion | bytes 6291456 | tf_op jit(solution)/shard_map/slice | solution.py:112
  382.4 8.8 %copy.44 = bf16[1,2,8,256,8,24]{5,4,3,2,1,0:T(8,128)(2,1)} copy(bf16[1,2,8,256,8,24]{5,4,2,1,0,3:T(8,128)(2,1)} %get-tuple-element.9) | data formatting | bytes 3145728 | tf_op jit(solution)/shard_map/slice | solution.py:112
  391.2 11.4 %multiply_reduce_fusion = (f32[16,128]{1,0:T(8,128)S(1)}, f32[16,128,2048]{2,1,0:T(8,128)}) fusion(bf16[16,128,24]{2,1,0:T(8,128)(2,1)S(1)} %bitcast.105, bf16[16,2048,24]{2,1,0:T(8,128)(2,1)} %bitcast.99), kind=kOutput, calls=%fused_computation.2 | convolution fusion | flops 209713152 | bytes 18456576 | tf_op jit(solution)/shard_map/nqd,nkd->nqk/dot_general | solution.py:35
  402.6 8.8 %copy.42 = bf16[1,2,8,256,8,24]{5,4,3,2,1,0:T(8,128)(2,1)} copy(bf16[1,2,8,256,8,24]{5,4,2,1,0,3:T(8,128)(2,1)} %get-tuple-element.10) | data formatting | bytes 3145728 | tf_op jit(solution)/shard_map/slice | solution.py:113
  411.4 7.7 %fusion.2 = f32[16,128]{1,0:T(8,128)S(1)} fusion(f32[16,128,2048]{2,1,0:T(8,128)} %get-tuple-element.16, f32[16,128]{1,0:T(8,128)S(1)} %broadcast_maximum_fusion), kind=kLoop, calls=%fused_computation.6 | loop fusion | flops 12580864 | bytes 16793600 | tf_op jit(solution)/shard_map/reduce_sum | solution.py:39
  419.6 7.9 %fusion.16 = bf16[16,24,128]{2,1,0:T(8,128)(2,1)S(1)} fusion(bf16[16,2048,24]{2,1,0:T(8,128)(2,1)S(1)} %bitcast.98, f32[16,128,2048]{2,1,0:T(8,128)} %get-tuple-element.16, f32[16,128]{1,0:T(8,128)S(1)} %broadcast_maximum_fusion, f32[16,128]{1,0:T(8,128)S(1)} %fusion.2), kind=kOutput, calls=%fused_computation.26 | convolution fusion | flops 214007808 | bytes 18464768 | tf_op jit(solution)/shard_map/nqk,nkd->ndq/dot_general | solution.py:40
  (78 shorter events, 30.4 us)
Async XLA Ops:
  6.5 50.3 %copy-start = (bf16[384,1152]{1,0:T(8,128)(2,1)S(1)}, bf16[384,1152]{1,0:T(8,128)(2,1)}, u32[]{:S(2)}) copy-start(bf16[384,1152]{1,0:T(8,128)(2,1)} %param.17) | copy-start | bytes 2654212
  6.5 47.9 %copy-start.8 = (f32[384]{0:T(512)S(1)}, f32[384]{0:T(512)}, u32[]{:S(2)}) copy-start(f32[384]{0:T(512)} %param.12) | copy-start | bytes 4612
  6.5 49.4 %copy-start.10 = (f32[384]{0:T(512)S(1)}, f32[384]{0:T(512)}, u32[]{:S(2)}) copy-start(f32[384]{0:T(512)} %param.13) | copy-start | bytes 4612
  6.5 49.4 %copy-start.9 = (f32[384]{0:T(512)S(1)}, f32[384]{0:T(512)}, u32[]{:S(2)}) copy-start(f32[384]{0:T(512)} %param.14) | copy-start | bytes 4612
  6.5 50.3 %copy-start.12 = (f32[384]{0:T(512)S(1)}, f32[384]{0:T(512)}, u32[]{:S(2)}) copy-start(f32[384]{0:T(512)} %param.15) | copy-start | bytes 4612
  6.5 50.3 %copy-start.11 = (f32[384]{0:T(512)S(1)}, f32[384]{0:T(512)}, u32[]{:S(2)}) copy-start(f32[384]{0:T(512)} %param.16) | copy-start | bytes 4612
  6.6 157.0 %all-gather.3.cloned.1.call-start = ((), (), s32[]{:S(2)}) async-start(), calls=%async_computation | async-start | bytes 17825792 | tf_op jit(solution)/shard_map/all_gather | solution.py:94
  7.4 30.3 %collective-permute-start = (bf16[1,32,192]{2,1,0:T(8,128)(2,1)S(1)}, bf16[1,32,192]{2,1,0:T(8,128)(2,1)S(1)}, u32[]{:S(2)}, u32[]{:S(2)}) collective-permute-start(bf16[1,32,192]{2,1,0:T(8,128)(2,1)S(1)} %slice.90), channel_id=1, source_target_pairs={{0,16},{16,32},{32,48},{48,64},{64,80},{80,96},{96,112},{112,128},... | collective-permute-start | bytes 36872 | tf_op jit(solution)/shard_map/ppermute | solution.py:15
  39.3 5.2 %collective-permute-start.1 = (bf16[33,1,192]{2,1,0:T(2,128)(2,1)S(1)}, bf16[33,1,192]{2,1,0:T(2,128)(2,1)S(1)}, u32[]{:S(2)}, u32[]{:S(2)}) collective-permute-start(bf16[33,1,192]{2,1,0:T(2,128)(2,1)S(1)} %slice.120), channel_id=1, source_target_pairs={{0,1},{1,2},{2,3},{3,4},{4,5},{5,6},{6,7},{7,8},{8,9},{9,10},{10,1... | collective-permute-start | bytes 38024 | tf_op jit(solution)/shard_map/ppermute | solution.py:15
  56.1 0.7 copy-start.4
  65.2 1.1 copy-start.3
  67.6 299.9 %all-gather.5.cloned.1.call-start = ((), (), s32[]{:S(2)}) async-start(), calls=%async_computation.1 | async-start | bytes 17825792 | tf_op jit(solution)/shard_map/all_gather | solution.py:110
  382.4 8.8 %copy-start.6 = (bf16[2,8,16,8,24]{4,3,2,1,0:T(8,128)(2,1)S(1)}, bf16[2,8,16,8,24]{4,3,2,1,0:T(8,128)(2,1)}, u32[]{:S(2)}) copy-start(bf16[2,8,16,8,24]{4,3,2,1,0:T(8,128)(2,1)} %copy.43) | copy-start | bytes 294916
  411.4 8.2 %copy-start.2 = (bf16[1,2,8,256,8,24]{5,4,3,2,1,0:T(8,128)(2,1)S(1)}, bf16[1,2,8,256,8,24]{5,4,3,2,1,0:T(8,128)(2,1)}, u32[]{:S(2)}) copy-start(bf16[1,2,8,256,8,24]{5,4,3,2,1,0:T(8,128)(2,1)} %copy.42) | copy-start | bytes 4718596
  419.6 10.2 %copy-start.5 = (bf16[256,384]{1,0:T(8,128)(2,1)S(1)}, bf16[256,384]{1,0:T(8,128)(2,1)}, u32[]{:S(2)}) copy-start(bf16[256,384]{1,0:T(8,128)(2,1)} %copy-done.4) | copy-start | bytes 589828
  419.6 10.2 %copy-start.7 = (bf16[384,384]{1,0:T(8,128)(2,1)S(1)}, bf16[384,384]{1,0:T(8,128)(2,1)}, u32[]{:S(2)}) copy-start(bf16[384,384]{1,0:T(8,128)(2,1)} %param.18) | copy-start | bytes 884740
  419.6 10.2 %copy-start.13 = (f32[384]{0:T(512)S(1)}, f32[384]{0:T(512)}, u32[]{:S(2)}) copy-start(f32[384]{0:T(512)} %param.19) | copy-start | bytes 4612
  419.6 11.2 %copy-start.1 = (bf16[384,1152]{1,0:T(8,128)(2,1)S(1)}, bf16[384,1152]{1,0:T(8,128)(2,1)}, u32[]{:S(2)}) copy-start(bf16[384,1152]{1,0:T(8,128)(2,1)} %param.17) | copy-start | bytes 2654212
Sparse Core Ops, SparseCore 0:
  67.7 95.7 all-gather.2
  165.9 201.5 all-gather.4
where the time goes:
time: 443 us; the launch traced here: 438 us
  waiting for transfers between devices  253 us (57%)
  local copies, waits for them, and re-layouts  112 us (25%)
  matrix products  39.1 us (9%)
  between operations  13.8 us (3%)
  other arithmetic  12.2 us (3%)
  starting transfers between devices  7.16 us (2%)
    all_gather x1, waiting for transfers between devices, on_device(): piece = lax.all_gather(col_pairs, 'row', axis=3, tiled=True)  160 us
    all_gather x1, waiting for transfers between devices, on_device(): piece = lax.all_gather(row_pairs, 'col', axis=4, tiled=True)  91.2 us
    slice x9, local copies, waits for them, and re-layouts, on_device(): padded[tap_row:tap_row + 2 * tile_rows:2, tap_col:tap_col + 2 * tile_cols:2]  27.6 us
    slice x2, local copies, waits for them, and re-layouts, on_device(): key_rows = piece[0].reshape(col_count * heads_half, span * stripe, depth)  23.7 us
    slice x2, local copies, waits for them, and re-layouts, on_device(): key_rows = piece[0].reshape(row_count * heads_half, stripe * span, depth)  19.3 us
    dot_general x2, matrix products, online_step(): jnp.einsum('nqd,nkd->nqk', queries, key_rows, preferred_element_type=jnp....  15.3 us
    dot_general x2, matrix products, online_step(): jnp.einsum('nqk,nkd->ndq', weights.astype(jnp.bfloat16), value_rows, pref...  12.1 us
    reduce_sum x2, other arithmetic, online_step(): totals = jnp.sum(weights, -1)  11 us
  transfers between devices with their start and end apart: 4, of which 3 were waited for; matrix products, arithmetic and copies ran while one was open for 17% of the time, Pallas kernels for 0%

commit v1 on v0

v1 whole, which is shorter than its diff:
```python
import functools
import math

import jax
import jax.numpy as jnp
from jax import lax
from jax.experimental import pallas as pl
from jax.experimental.pallas import tpu as pltpu
from jax.sharding import PartitionSpec as P

HEADS = 16
SPLIT = 8
PEERS = 16
DEPTH = 24
BLOCK = 80
BACK = 32
HALF = 192
DIM = 384
TOKENS = 256
F32 = jnp.float32
BF16 = jnp.bfloat16
MESH = pl.DeviceIdType.MESH


def layer_norm(values, gain, shift):
    center = values - jnp.mean(values, -1, keepdims=True)
    spread = jnp.mean(center * center, -1, keepdims=True)
    return center * lax.rsqrt(spread + 1e-05) * gain + shift


def by_stripe(values):
    pieces = [values[16 * i + 8 * s : 16 * i + 8 * s + 8] for s in range(2) for i in range(16)]
    return jnp.concatenate(pieces, 0)


def by_row(values):
    pieces = [values[128 * s + 8 * i : 128 * s + 8 * i + 8] for i in range(16) for s in range(2)]
    return jnp.concatenate(pieces, 0)


def kernel(
    image_hbm, conv_hbm, qkv_hbm, proj_hbm,
    conv_bias, merge_gain, merge_shift, norm_gain, norm_shift, proj_bias,
    out_ref,
    image, conv_w, qkv_w, proj_w, padded, phases, qkv_t,
    column, halo_row, halo_col, halo_corner,
    send_r, recv_r, send_c, recv_c,
    back_send_r, back_recv_r, back_send_c, back_recv_c,
    query_t, keys, value_t, scores, tokens_ref,
    load_sem, halo_send, halo_recv,
    send_sem, recv_sem, back_send_sem, back_recv_sem,
):
    me_r = lax.axis_index("row")
    me_c = lax.axis_index("col")
    down, up = lax.rem(me_r + 1, PEERS), lax.rem(me_r + PEERS - 1, PEERS)
    right, left = lax.rem(me_c + 1, PEERS), lax.rem(me_c + PEERS - 1, PEERS)

    loads = [
        pltpu.make_async_copy(image_hbm, image, load_sem.at[0]),
        pltpu.make_async_copy(qkv_hbm, qkv_w, load_sem.at[1]),
        pltpu.make_async_copy(conv_hbm, conv_w, load_sem.at[2]),
        pltpu.make_async_copy(proj_hbm, proj_w, load_sem.at[3]),
    ]
    for load in loads:
        load.start()

    barrier = pltpu.get_barrier_semaphore()
    for step in range(1, PEERS):
        pl.semaphore_signal(barrier, inc=1, device_id=(me_r, lax.rem(me_c + step, PEERS)), device_id_type=MESH)
        pl.semaphore_signal(barrier, inc=1, device_id=(lax.rem(me_r + step, PEERS), me_c), device_id_type=MESH)
    pl.semaphore_signal(barrier, inc=1, device_id=(down, right), device_id_type=MESH)
    pl.semaphore_signal(barrier, inc=1, device_id=(up, left), device_id_type=MESH)

    loads[0].wait()
    def pad(rows, cols, values):
        padded[0, rows, cols, :] = values[:, :, 0:128]
        padded[1, rows, cols, 0:64] = values[:, :, 128:192]

    pad(slice(1, 33), slice(8, 40), image[...].astype(F32))
    column[:, 0:128] = padded[0, 1:33, 39:40, :].reshape(32, 128).astype(BF16)
    column[:, 128:192] = padded[1, 1:33, 39:40, 0:64].reshape(32, 64).astype(BF16)
    loads[1].wait()
    qkv_t[...] = qkv_w[...].T

    pl.semaphore_wait(barrier, 2 * (PEERS - 1) + 2)
    halos = [
        pltpu.make_async_remote_copy(
            src_ref=image.at[31], dst_ref=halo_row, send_sem=halo_send.at[0], recv_sem=halo_recv.at[0],
            device_id=(down, me_c), device_id_type=MESH),
        pltpu.make_async_remote_copy(
            src_ref=column, dst_ref=halo_col, send_sem=halo_send.at[1], recv_sem=halo_recv.at[1],
            device_id=(me_r, right), device_id_type=MESH),
        pltpu.make_async_remote_copy(
            src_ref=column.at[pl.ds(16, 16)], dst_ref=halo_corner, send_sem=halo_send.at[2], recv_sem=halo_recv.at[2],
            device_id=(down, right), device_id_type=MESH),
    ]
    for halo in halos:
        halo.start()
    loads[2].wait()
    loads[3].wait()
    for halo in halos:
        halo.wait()

    has_up, has_left = me_r > 0, me_c > 0
    pad(slice(0, 1), slice(8, 40), jnp.where(has_up, halo_row[...].astype(F32), 0.0)[None])
    pad(slice(1, 33), slice(7, 8), jnp.where(has_left, halo_col[...].astype(F32), 0.0).reshape(32, 1, 192))
    corner = halo_corner[...].astype(F32)[15:16]
    pad(slice(0, 1), slice(7, 8), jnp.where(jnp.logical_and(has_up, has_left), corner, 0.0)[None])
    for tap in range(3):
        low = padded[0, :, pl.ds(7 + tap, 16, stride=2), :].astype(BF16)
        high = padded[1, :, pl.ds(7 + tap, 16, stride=2), :].astype(BF16)
        phases[tap, :, :, :, 0:128] = low.reshape(17, 2, 16, 128)
        phases[tap, :, :, :, 128:192] = high[:, :, 0:64].reshape(17, 2, 16, 64)
    merged = jnp.zeros((TOKENS, DIM), F32)
    for a in range(3):
        for b in range(3):
            window = phases[b, pl.ds(a // 2, 16), a % 2].reshape(TOKENS, 192)
            merged = merged + jnp.dot(window, conv_w[a, b], preferred_element_type=F32)
    merged = merged + conv_bias[...][None, :]
    tokens = layer_norm(merged, merge_gain[...][None, :], merge_shift[...][None, :]).astype(BF16)
    tokens_ref[...] = tokens
    normed = layer_norm(tokens.astype(F32), norm_gain[...][None, :], norm_shift[...][None, :])

    ones = jnp.ones((8, TOKENS), F32)

    def project(normed_half, base, send):
        parts = [
            lax.dot_general(
                qkv_t[part * DIM + base : part * DIM + base + HALF, :], normed_half,
                (((1,), (1,)), ((), ())), preferred_element_type=F32)
            for part in range(3)
        ]
        for head in range(HEADS // 2):
            rows = slice(DEPTH * head, DEPTH * head + DEPTH)
            block = jnp.concatenate([part[rows] for part in parts] + [ones], 0).astype(BF16)
            send[head] = block[:, :128]
            send[8 + head] = block[:, 128:]

    def leave(axis, me, send, recv, phase, sends, recvs, peer):
        return pltpu.make_async_remote_copy(
            src_ref=send.at[peer], dst_ref=recv.at[me],
            send_sem=sends.at[phase, peer], recv_sem=recvs.at[phase, me],
            device_id=(me_r, peer) if axis == "col" else (peer, me_c), device_id_type=MESH)

    def arrive(axis, me, send, recv, phase, sends, recvs, peer):
        return pltpu.make_async_remote_copy(
            src_ref=send.at[peer], dst_ref=recv.at[peer],
            send_sem=sends.at[phase, peer], recv_sem=recvs.at[phase, peer],
            device_id=(me_r, peer) if axis == "col" else (peer, me_c), device_id_type=MESH)

    def start_all(axis, me, send, recv, phase):
        for step in range(1, PEERS):
            peer = lax.rem(me + step, PEERS)
            leave(axis, me, send, recv, phase, send_sem, recv_sem, peer).start()

    def wait_all(axis, me, send, recv, phase, sends, recvs, sent):
        for step in range(1, PEERS):
            peer = lax.rem(me + step, PEERS)
            if sent:
                leave(axis, me, send, recv, phase, sends, recvs, peer).wait_send()
            else:
                arrive(axis, me, send, recv, phase, sends, recvs, peer).wait_recv()

    project(normed.astype(BF16), 0, send_r)
    start_all("col", me_c, send_r, recv_r, 0)
    project(by_stripe(normed).astype(BF16), HALF, send_c)
    start_all("row", me_r, send_c, recv_c, 1)

    def attend(axis, me, send, recv, back_send, back_recv, phase):
        recv[me] = send[me]
        wait_all(axis, me, send, recv, phase, send_sem, recv_sem, False)
        for peer in range(PEERS):
            lanes = slice(128 * peer, 128 * peer + 128)
            query_t[:, lanes] = recv[peer, 0:32, :]
            value_t[:, lanes] = recv[peer, 48:80, :]
            own = recv[peer, 0:48, :].astype(F32)[24:48]
            own = jnp.concatenate([own, jnp.zeros((104, 128), F32)], 0)
            keys[lanes, :] = own.T.astype(BF16)
        mine = me // 2

        def tile(step, carry):
            place = lax.rem(mine + 1 + step, 8)
            start = pl.multiple_of(place * 256, 256)
            query = query_t[:, pl.ds(start, 256)]
            highest = jnp.full((8, 256), -jnp.inf, F32)
            for chunk in range(8):
                rows = slice(256 * chunk, 256 * chunk + 256)
                part = jnp.dot(keys[rows, 0:32], query, preferred_element_type=F32)
                scores[rows, :] = part
                highest = jnp.maximum(highest, jnp.max(part.reshape(32, 8, 256), 0))
            highest = jnp.max(highest, 0, keepdims=True)
            summed = jnp.zeros((32, 256), F32)
            for chunk in range(8):
                rows = slice(256 * chunk, 256 * chunk + 256)
                weights = jnp.exp((scores[rows, :] - highest) * (1.0 / math.sqrt(DEPTH)))
                summed = summed + jnp.dot(value_t[:, rows], weights.astype(BF16), preferred_element_type=F32)
            result = summed[0:24] / summed[24:25]
            result = jnp.concatenate([result, jnp.zeros((8, 256), F32)], 0).astype(BF16)
            back_send[2 * place] = result[:, :128]
            back_send[2 * place + 1] = result[:, 128:]
            for half in range(2):
                peer = 2 * place + half

                @pl.when(peer != me)
                def _():
                    leave(axis, me, back_send, back_recv, phase, back_send_sem, back_recv_sem, peer).start()

            return carry

        lax.fori_loop(0, 8, tile, 0)
        back_recv[me] = back_send[me]

    def mix(back_recv, base):
        outs = []
        for stripe in range(2):
            heads = [back_recv[8 * stripe + head].astype(F32)[0:24] for head in range(8)]
            mixed = jnp.concatenate(heads, 0).T.astype(BF16)
            outs.append(jnp.dot(mixed, proj_w[base : base + HALF, :], preferred_element_type=F32))
        return jnp.concatenate(outs, 0)

    attend("col", me_c, send_r, recv_r, back_send_r, back_recv_r, 0)
    attend("row", me_r, send_c, recv_c, back_send_c, back_recv_c, 1)
    wait_all("col", me_c, back_send_r, back_recv_r, 0, back_send_sem, back_recv_sem, False)
    total = mix(back_recv_r, 0) + tokens_ref[...].astype(F32) + proj_bias[...][None, :]
    wait_all("row", me_r, back_send_c, back_recv_c, 1, back_send_sem, back_recv_sem, False)
    total = (total + by_row(mix(back_recv_c, HALF))).astype(BF16)
    out_ref[...] = total.reshape(16, 16, DIM)
    wait_all("col", me_c, send_r, recv_r, 0, send_sem, recv_sem, True)
    wait_all("row", me_r, send_c, recv_c, 1, send_sem, recv_sem, True)
    wait_all("col", me_c, back_send_r, back_recv_r, 0, back_send_sem, back_recv_sem, True)
    wait_all("row", me_r, back_send_c, back_recv_c, 1, back_send_sem, back_recv_sem, True)


def on_device(image, conv_weight, conv_bias, merge_gain, merge_shift, norm_gain, norm_shift, qkv_weight, proj_weight, proj_bias):
    anyspace = pl.BlockSpec(memory_space=pl.ANY)
    vmem = pl.BlockSpec(memory_space=pltpu.VMEM)
    return pl.pallas_call(
        kernel,
        out_shape=jax.ShapeDtypeStruct((16, 16, DIM), BF16),
        in_specs=[anyspace] * 4 + [vmem] * 6,
        out_specs=vmem,
        scratch_shapes=[
            pltpu.VMEM((32, 32, 192), BF16),
            pltpu.VMEM((3, 3, 192, DIM), BF16),
            pltpu.VMEM((DIM, 3 * DIM), BF16),
            pltpu.VMEM((DIM, DIM), BF16),
            pltpu.VMEM((2, 34, 40, 128), F32),
            pltpu.VMEM((3, 17, 2, 16, 192), BF16),
            pltpu.VMEM((3 * DIM, DIM), BF16),
            pltpu.VMEM((32, 192), BF16),
            pltpu.VMEM((32, 192), BF16),
            pltpu.VMEM((32, 192), BF16),
            pltpu.VMEM((16, 192), BF16),
        ]
        + [pltpu.VMEM((PEERS, BLOCK, 128), BF16)] * 4
        + [pltpu.VMEM((PEERS, BACK, 128), BF16)] * 4
        + [
            pltpu.VMEM((32, 2048), BF16),
            pltpu.VMEM((2048, 128), BF16),
            pltpu.VMEM((32, 2048), BF16),
            pltpu.VMEM((2048, 256), F32),
            pltpu.VMEM((TOKENS, DIM), BF16),
            pltpu.SemaphoreType.DMA((4,)),
            pltpu.SemaphoreType.DMA((3,)),
            pltpu.SemaphoreType.DMA((3,)),
            pltpu.SemaphoreType.DMA((2, PEERS)),
            pltpu.SemaphoreType.DMA((2, PEERS)),
            pltpu.SemaphoreType.DMA((2, PEERS)),
            pltpu.SemaphoreType.DMA((2, PEERS)),
        ],
        compiler_params=pltpu.CompilerParams(
            collective_id=0, has_side_effects=True, vmem_limit_bytes=48 << 20),
    )(image, conv_weight, qkv_weight, proj_weight, conv_bias, merge_gain, merge_shift, norm_gain, norm_shift, proj_bias)


def solution(mesh):
    return jax.shard_map(
        on_device,
        mesh=mesh,
        in_specs=(P("row", "col", None), P(), P(), P(), P(), P(), P(), P(), P(), P()),
        out_specs=P("row", "col", None),
        check_vma=False,
    )
```

time: 443 us -> 55 us (0.12); the launches traced: 438 us -> 54.6 us
  waiting for transfers between devices: 253 us -> 0 us
  local copies, waits for them, and re-layouts: 112 us -> 9.26 us
  Pallas kernels: 0 us -> 45.3 us
  matrix products: 39.1 us -> 0 us
  between operations: 13.8 us -> 0.02 us
  other arithmetic: 12.2 us -> 0 us
  starting transfers between devices: 7.16 us -> 0 us
    all_gather x2 -> x0, waiting for transfers between devices: 252 us -> none  [the longest x1 160 us: on_device(): piece = lax.all_gather(col_pairs, 'row', axis=3, tiled=True)]
    slice x18 -> x0, local copies, waits for them, and re-layouts: 90.2 us -> none  [the longest x9 27.6 us: on_device(): padded[tap_row:tap_row + 2 * tile_rows:2, tap_col:tap_col + 2 * tile_cols:2]]
    pallas_call x0 -> x1, Pallas kernels: none -> 45.3 us  [on_device(): pl.pallas_call(kernel, out_shape=jax.ShapeDtypeStruct((16, 16, DIM), BF16...]
    dot_general x15 -> x0, matrix products: 39.1 us -> none  [the longest x2 15.3 us: online_step(): jnp.einsum('nqd,nkd->nqk', queries, key_rows, preferred_element_type=jnp....]
    reduce_sum x5 -> x0, other arithmetic: 11.6 us -> none  [the longest x2 11 us: online_step(): totals = jnp.sum(weights, -1)]
    reshape x4 -> x0, local copies, waits for them, and re-layouts: 7.58 us -> none  [the longest x1 5.44 us: on_device(): projected = projected.reshape(tile_rows, tile_cols, 3, 2, heads_half, depth)]
    unnamed x29 -> x21, local copies, waits for them, and re-layouts: 2.16 us -> 9.26 us
    ppermute x2 -> x0, starting transfers between devices: 7.08 us -> none  [shifted(): lax.ppermute(value, axis, [(source, source + steps) for source in range(i...]
  transfers between devices with their start and end apart: 4 -> 0, of which waited for: 3 -> 0; matrix products, arithmetic and copies ran while one was open for 17% -> 0% of each run, Pallas kernels for 0% -> 0%
where the time goes in v1:
time: 55 us; the launch traced here: 54.6 us
  Pallas kernels  45.3 us (82%)
  local copies, waits for them, and re-layouts  9.26 us (17%)
    pallas_call x1, Pallas kernels, on_device(): pl.pallas_call(kernel, out_shape=jax.ShapeDtypeStruct((16, 16, DIM), BF16...  45.3 us
    unnamed x21, local copies, waits for them, and re-layouts  9.26 us

profile of v1, /device:TPU:32, one launch (start us, length us, event | category | flops | bytes accessed | tf_op | source)
XLA Modules:
  0.0 54.6 jit_solution(5356942165216773507)
XLA Ops:
  0.0 0.0 copy-start
  0.0 1.3 %copy-done = bf16[3,3,192,384]{3,2,1,0:T(8,128)(2,1)S(1)} copy-done((bf16[3,3,192,384]{3,2,1,0:T(8,128)(2,1)S(1)}, bf16[3,3,192,384]{3,2,1,0:T(8,128)(2,1)}, u32[]{:S(2)}) %copy-start) | copy-done | bytes 1327128
  1.3 0.0 copy-start.1
  1.3 1.2 %copy-done.1 = bf16[384,1152]{1,0:T(8,128)(2,1)S(1)} copy-done((bf16[384,1152]{1,0:T(8,128)(2,1)S(1)}, bf16[384,1152]{1,0:T(8,128)(2,1)}, u32[]{:S(2)}) %copy-start.1) | copy-done | bytes 884760
  2.5 0.0 copy-start.2
  2.5 1.0 %copy-done.2 = bf16[32,32,192]{2,1,0:T(8,128)(2,1)S(1)} copy-done((bf16[32,32,192]{2,1,0:T(8,128)(2,1)S(1)}, bf16[32,32,192]{2,1,0:T(8,128)(2,1)}, u32[]{:S(2)}) %copy-start.2) | copy-done | bytes 393240
  3.5 0.0 copy-start.3
  3.5 1.0 %copy-done.3 = bf16[384,384]{1,0:T(8,128)(2,1)S(1)} copy-done((bf16[384,384]{1,0:T(8,128)(2,1)S(1)}, bf16[384,384]{1,0:T(8,128)(2,1)}, u32[]{:S(2)}) %copy-start.3) | copy-done | bytes 294936
  4.5 0.0 copy-start.4
  4.5 0.7 %copy-done.4 = f32[384]{0:T(512)S(1)} copy-done((f32[384]{0:T(512)S(1)}, f32[384]{0:T(512)}, u32[]{:S(2)}) %copy-start.4) | copy-done | bytes 1560
  5.2 0.0 copy-start.5
  5.2 0.7 %copy-done.5 = f32[384]{0:T(512)S(1)} copy-done((f32[384]{0:T(512)S(1)}, f32[384]{0:T(512)}, u32[]{:S(2)}) %copy-start.5) | copy-done | bytes 1560
  5.9 0.0 copy-start.6
  5.9 0.7 %copy-done.6 = f32[384]{0:T(512)S(1)} copy-done((f32[384]{0:T(512)S(1)}, f32[384]{0:T(512)}, u32[]{:S(2)}) %copy-start.6) | copy-done | bytes 1560
  6.5 0.0 copy-start.7
  6.5 0.7 %copy-done.7 = f32[384]{0:T(512)S(1)} copy-done((f32[384]{0:T(512)S(1)}, f32[384]{0:T(512)}, u32[]{:S(2)}) %copy-start.7) | copy-done | bytes 1560
  7.2 0.0 copy-start.8
  7.2 0.7 %copy-done.8 = f32[384]{0:T(512)S(1)} copy-done((f32[384]{0:T(512)S(1)}, f32[384]{0:T(512)}, u32[]{:S(2)}) %copy-start.8) | copy-done | bytes 1560
  7.9 0.0 copy-start.9
  7.9 0.7 %copy-done.9 = f32[384]{0:T(512)S(1)} copy-done((f32[384]{0:T(512)S(1)}, f32[384]{0:T(512)}, u32[]{:S(2)}) %copy-start.9) | copy-done | bytes 1560
  8.6 45.3 %shard_map.100 = bf16[16,16,384]{2,1,0:T(8,128)(2,1)S(1)} custom-call(bf16[32,32,192]{2,1,0:T(8,128)(2,1)S(1)} %copy-done.2, bf16[3,3,192,384]{3,2,1,0:T(8,128)(2,1)S(1)} %copy-done, bf16[384,1152]{1,0:T(8,128)(2,1)S(1)} %copy-done.1, bf16[384,384]{1,0:T(8,128)(2,1)S(1)} %copy-done.3, f32[384]{0:T(512)S(1)} %copy-done.4, f32[384]{0:T(512)S(1)} %copy-done.5, ...), custom_call_target="tpu_custom_call" | custom-call | tf_op jit(solution)/shard_map/pallas_call | solution.py:237
  53.9 0.7 %copy.12 = bf16[16,16,384]{2,1,0:T(8,128)(2,1)} copy(bf16[16,16,384]{2,1,0:T(8,128)(2,1)S(1)} %shard_map.100) | data formatting | bytes 393216
Async XLA Ops:
  0.0 1.3 %copy-start = (bf16[3,3,192,384]{3,2,1,0:T(8,128)(2,1)S(1)}, bf16[3,3,192,384]{3,2,1,0:T(8,128)(2,1)}, u32[]{:S(2)}) copy-start(bf16[3,3,192,384]{3,2,1,0:T(8,128)(2,1)} %conv_hbm.1) | copy-start | bytes 3981316
  1.3 1.2 %copy-start.1 = (bf16[384,1152]{1,0:T(8,128)(2,1)S(1)}, bf16[384,1152]{1,0:T(8,128)(2,1)}, u32[]{:S(2)}) copy-start(bf16[384,1152]{1,0:T(8,128)(2,1)} %qkv_hbm.1) | copy-start | bytes 2654212
  2.5 1.0 %copy-start.2 = (bf16[32,32,192]{2,1,0:T(8,128)(2,1)S(1)}, bf16[32,32,192]{2,1,0:T(8,128)(2,1)}, u32[]{:S(2)}) copy-start(bf16[32,32,192]{2,1,0:T(8,128)(2,1)} %image_hbm.1) | copy-start | bytes 1179652
  3.5 1.0 %copy-start.3 = (bf16[384,384]{1,0:T(8,128)(2,1)S(1)}, bf16[384,384]{1,0:T(8,128)(2,1)}, u32[]{:S(2)}) copy-start(bf16[384,384]{1,0:T(8,128)(2,1)} %proj_hbm.1) | copy-start | bytes 884740
  4.5 0.7 %copy-start.4 = (f32[384]{0:T(512)S(1)}, f32[384]{0:T(512)}, u32[]{:S(2)}) copy-start(f32[384]{0:T(512)} %conv_bias.1) | copy-start | bytes 4612
  5.2 0.7 %copy-start.5 = (f32[384]{0:T(512)S(1)}, f32[384]{0:T(512)}, u32[]{:S(2)}) copy-start(f32[384]{0:T(512)} %merge_gain.1) | copy-start | bytes 4612
  5.9 0.7 %copy-start.6 = (f32[384]{0:T(512)S(1)}, f32[384]{0:T(512)}, u32[]{:S(2)}) copy-start(f32[384]{0:T(512)} %merge_shift.1) | copy-start | bytes 4612
  6.5 0.7 %copy-start.7 = (f32[384]{0:T(512)S(1)}, f32[384]{0:T(512)}, u32[]{:S(2)}) copy-start(f32[384]{0:T(512)} %norm_gain.1) | copy-start | bytes 4612
  7.2 0.7 %copy-start.8 = (f32[384]{0:T(512)S(1)}, f32[384]{0:T(512)}, u32[]{:S(2)}) copy-start(f32[384]{0:T(512)} %norm_shift.1) | copy-start | bytes 4612
  7.9 0.7 %copy-start.9 = (f32[384]{0:T(512)S(1)}, f32[384]{0:T(512)}, u32[]{:S(2)}) copy-start(f32[384]{0:T(512)} %proj_bias.1) | copy-start | bytes 4612

commit v2 on v1

--- a/solution.py
+++ b/solution.py
@@ -12,10 +12,11 @@
 SPLIT = 8
 PEERS = 16
 DEPTH = 24
-BLOCK = 80
-BACK = 32
+BLOCK = 72
+BACK = 24
 HALF = 192
 DIM = 384
+CHUNK = 512
 TOKENS = 256
 F32 = jnp.float32
 BF16 = jnp.bfloat16
@@ -40,8 +41,9 @@
 
 def kernel(
     image_hbm, conv_hbm, qkv_hbm, proj_hbm,
+    conv_bias_hbm, merge_gain_hbm, merge_shift_hbm, norm_gain_hbm, norm_shift_hbm, proj_bias_hbm,
+    out_ref,
     conv_bias, merge_gain, merge_shift, norm_gain, norm_shift, proj_bias,
-    out_ref,
     image, conv_w, qkv_w, proj_w, padded, phases, qkv_t,
     column, halo_row, halo_col, halo_corner,
     send_r, recv_r, send_c, recv_c,
@@ -55,21 +57,27 @@
     down, up = lax.rem(me_r + 1, PEERS), lax.rem(me_r + PEERS - 1, PEERS)
     right, left = lax.rem(me_c + 1, PEERS), lax.rem(me_c + PEERS - 1, PEERS)
 
+    barrier = pltpu.get_barrier_semaphore()
+    for step in range(1, PEERS):
+        pl.semaphore_signal(barrier, inc=1, device_id=(me_r, lax.rem(me_c + step, PEERS)), device_id_type=MESH)
+        pl.semaphore_signal(barrier, inc=1, device_id=(lax.rem(me_r + step, PEERS), me_c), device_id_type=MESH)
+    pl.semaphore_signal(barrier, inc=1, device_id=(down, right), device_id_type=MESH)
+    pl.semaphore_signal(barrier, inc=1, device_id=(up, left), device_id_type=MESH)
+
     loads = [
         pltpu.make_async_copy(image_hbm, image, load_sem.at[0]),
         pltpu.make_async_copy(qkv_hbm, qkv_w, load_sem.at[1]),
         pltpu.make_async_copy(conv_hbm, conv_w, load_sem.at[2]),
         pltpu.make_async_copy(proj_hbm, proj_w, load_sem.at[3]),
     ]
-    for load in loads:
+    vectors = [
+        pltpu.make_async_copy(source, target, load_sem.at[4 + place])
+        for place, (source, target) in enumerate([
+            (conv_bias_hbm, conv_bias), (merge_gain_hbm, merge_gain), (merge_shift_hbm, merge_shift),
+            (norm_gain_hbm, norm_gain), (norm_shift_hbm, norm_shift), (proj_bias_hbm, proj_bias)])
+    ]
+    for load in loads + vectors:
         load.start()
-
-    barrier = pltpu.get_barrier_semaphore()
-    for step in range(1, PEERS):
-        pl.semaphore_signal(barrier, inc=1, device_id=(me_r, lax.rem(me_c + step, PEERS)), device_id_type=MESH)
-        pl.semaphore_signal(barrier, inc=1, device_id=(lax.rem(me_r + step, PEERS), me_c), device_id_type=MESH)
-    pl.semaphore_signal(barrier, inc=1, device_id=(down, right), device_id_type=MESH)
-    pl.semaphore_signal(barrier, inc=1, device_id=(up, left), device_id_type=MESH)
 
     loads[0].wait()
     def pad(rows, cols, values):
@@ -81,6 +89,7 @@
     column[:, 128:192] = padded[1, 1:33, 39:40, 0:64].reshape(32, 64).astype(BF16)
     loads[1].wait()
     qkv_t[...] = qkv_w[...].T
+    value_t[24:32, :] = jnp.ones((8, 2048), BF16)
 
     pl.semaphore_wait(barrier, 2 * (PEERS - 1) + 2)
     halos = [
@@ -96,8 +105,8 @@
     ]
     for halo in halos:
         halo.start()
-    loads[2].wait()
-    loads[3].wait()
+    for load in loads[2:] + vectors:
+        load.wait()
     for halo in halos:
         halo.wait()
 
@@ -121,8 +130,6 @@
     tokens_ref[...] = tokens
     normed = layer_norm(tokens.astype(F32), norm_gain[...][None, :], norm_shift[...][None, :])
 
-    ones = jnp.ones((8, TOKENS), F32)
-
     def project(normed_half, base, send):
         parts = [
             lax.dot_general(
@@ -132,7 +139,7 @@
         ]
         for head in range(HEADS // 2):
             rows = slice(DEPTH * head, DEPTH * head + DEPTH)
-            block = jnp.concatenate([part[rows] for part in parts] + [ones], 0).astype(BF16)
+            block = jnp.concatenate([part[rows] for part in parts], 0).astype(BF16)
             send[head] = block[:, :128]
             send[8 + head] = block[:, 128:]
 
@@ -172,30 +179,29 @@
         for peer in range(PEERS):
             lanes = slice(128 * peer, 128 * peer + 128)
             query_t[:, lanes] = recv[peer, 0:32, :]
-            value_t[:, lanes] = recv[peer, 48:80, :]
+            value_t[0:24, lanes] = recv[peer, 48:72, :]
             own = recv[peer, 0:48, :].astype(F32)[24:48]
             own = jnp.concatenate([own, jnp.zeros((104, 128), F32)], 0)
             keys[lanes, :] = own.T.astype(BF16)
-        mine = me // 2
-
-        def tile(step, carry):
-            place = lax.rem(mine + 1 + step, 8)
-            start = pl.multiple_of(place * 256, 256)
-            query = query_t[:, pl.ds(start, 256)]
-            highest = jnp.full((8, 256), -jnp.inf, F32)
-            for chunk in range(8):
-                rows = slice(256 * chunk, 256 * chunk + 256)
-                part = jnp.dot(keys[rows, 0:32], query, preferred_element_type=F32)
-                scores[rows, :] = part
-                highest = jnp.maximum(highest, jnp.max(part.reshape(32, 8, 256), 0))
-            highest = jnp.max(highest, 0, keepdims=True)
-            summed = jnp.zeros((32, 256), F32)
-            for chunk in range(8):
-                rows = slice(256 * chunk, 256 * chunk + 256)
-                weights = jnp.exp((scores[rows, :] - highest) * (1.0 / math.sqrt(DEPTH)))
-                summed = summed + jnp.dot(value_t[:, rows], weights.astype(BF16), preferred_element_type=F32)
-            result = summed[0:24] / summed[24:25]
-            result = jnp.concatenate([result, jnp.zeros((8, 256), F32)], 0).astype(BF16)
+        outer, inner = (me // 4, lax.rem(me // 2, 2)) if axis == "col" else (me // 4, lax.rem(me, 4) // 2)
+        places = []
+        for inner_step in (1, 0):
+            for outer_step in (2, 1, 3, 0):
+                places.append(lax.rem(outer + outer_step, 4) * 2 + lax.rem(inner + inner_step, 2))
+
+        def score(query, buffer, chunk, highest):
+            rows = slice(CHUNK * chunk, CHUNK * chunk + CHUNK)
+            part = jnp.dot(keys[rows, 0:32], query, preferred_element_type=F32)
+            scores[buffer, rows, :] = part
+            return jnp.maximum(highest, jnp.max(part.reshape(CHUNK // 8, 8, 256), 0))
+
+        def gather(buffer, chunk, highest, summed):
+            rows = slice(CHUNK * chunk, CHUNK * chunk + CHUNK)
+            weights = jnp.exp2((scores[buffer, rows, :] - highest) * (math.log2(math.e) / math.sqrt(DEPTH)))
+            return summed + jnp.dot(value_t[:, rows], weights.astype(BF16), preferred_element_type=F32)
+
+        def finish(place, summed):
+            result = (summed[0:24] / summed[24:25]).astype(BF16)
             back_send[2 * place] = result[:, :128]
             back_send[2 * place + 1] = result[:, 128:]
             for half in range(2):
@@ -205,15 +211,26 @@
                 def _():
                     leave(axis, me, back_send, back_recv, phase, back_send_sem, back_recv_sem, peer).start()
 
-            return carry
-
-        lax.fori_loop(0, 8, tile, 0)
+        highest = None
+        for step in range(9):
+            later = jnp.full((8, 256), -jnp.inf, F32)
+            summed = jnp.zeros((32, 256), F32)
+            if step < 8:
+                query = query_t[:, pl.ds(pl.multiple_of(places[step] * 256, 256), 256)]
+            for chunk in range(2048 // CHUNK):
+                if step < 8:
+                    later = score(query, step % 2, chunk, later)
+                if step > 0:
+                    summed = gather((step - 1) % 2, chunk, highest, summed)
+            if step > 0:
+                finish(places[step - 1], summed)
+            highest = jnp.max(later, 0, keepdims=True)
         back_recv[me] = back_send[me]
 
     def mix(back_recv, base):
         outs = []
         for stripe in range(2):
-            heads = [back_recv[8 * stripe + head].astype(F32)[0:24] for head in range(8)]
+            heads = [back_recv[8 * stripe + head].astype(F32) for head in range(8)]
             mixed = jnp.concatenate(heads, 0).T.astype(BF16)
             outs.append(jnp.dot(mixed, proj_w[base : base + HALF, :], preferred_element_type=F32))
         return jnp.concatenate(outs, 0)
@@ -232,14 +249,15 @@
 
 
 def on_device(image, conv_weight, conv_bias, merge_gain, merge_shift, norm_gain, norm_shift, qkv_weight, proj_weight, proj_bias):
-    anyspace = pl.BlockSpec(memory_space=pl.ANY)
+    anyspace = pl.BlockSpec(memory_space=pltpu.HBM)
     vmem = pl.BlockSpec(memory_space=pltpu.VMEM)
     return pl.pallas_call(
         kernel,
         out_shape=jax.ShapeDtypeStruct((16, 16, DIM), BF16),
-        in_specs=[anyspace] * 4 + [vmem] * 6,
+        in_specs=[anyspace] * 10,
         out_specs=vmem,
-        scratch_shapes=[
+        scratch_shapes=[pltpu.VMEM((DIM,), F32)] * 6
+        + [
             pltpu.VMEM((32, 32, 192), BF16),
             pltpu.VMEM((3, 3, 192, DIM), BF16),
             pltpu.VMEM((DIM, 3 * DIM), BF16),
@@ -258,9 +276,9 @@
             pltpu.VMEM((32, 2048), BF16),
             pltpu.VMEM((2048, 128), BF16),
             pltpu.VMEM((32, 2048), BF16),
-            pltpu.VMEM((2048, 256), F32),
+            pltpu.VMEM((2, 2048, 256), F32),
             pltpu.VMEM((TOKENS, DIM), BF16),
-            pltpu.SemaphoreType.DMA((4,)),
+            pltpu.SemaphoreType.DMA((10,)),
             pltpu.SemaphoreType.DMA((3,)),
             pltpu.SemaphoreType.DMA((3,)),
             pltpu.SemaphoreType.DMA((2, PEERS)),
@@ -269,7 +287,7 @@
             pltpu.SemaphoreType.DMA((2, PEERS)),
         ],
         compiler_params=pltpu.CompilerParams(
-            collective_id=0, has_side_effects=True, vmem_limit_bytes=48 << 20),
+            collective_id=0, has_side_effects=True, vmem_limit_bytes=67043328),
     )(image, conv_weight, qkv_weight, proj_weight, conv_bias, merge_gain, merge_shift, norm_gain, norm_shift, proj_bias)
 
 

time: 55 us -> 41 us (0.75)
  local copies, waits for them, and re-layouts: 9.26 us -> 1.62 us
  Pallas kernels: 45.3 us -> 38.8 us
    unnamed x21 -> x1, local copies, waits for them, and re-layouts: 9.26 us -> 1.62 us
    pallas_call x1, Pallas kernels: 45.3 us -> 38.8 us  [on_device(): pl.pallas_call(kernel, out_shape=jax.ShapeDtypeStruct((16, 16, DIM), BF16...]
where the time goes in v2:
time: 41 us; the launch traced here: 40.5 us
  Pallas kernels  38.8 us (95%)
  local copies, waits for them, and re-layouts  1.62 us (4%)
    pallas_call x1, Pallas kernels, on_device(): pl.pallas_call(kernel, out_shape=jax.ShapeDtypeStruct((16, 16, DIM), BF16...  38.8 us
    unnamed x1, local copies, waits for them, and re-layouts  1.62 us

profile of v2, /device:TPU:32, one launch (start us, length us, event | category | flops | bytes accessed | tf_op | source)
XLA Modules:
  0.0 40.5 jit_solution(11096093685901333565)
XLA Ops:
  0.0 38.8 %shard_map.100 = bf16[16,16,384]{2,1,0:T(8,128)(2,1)} custom-call(bf16[32,32,192]{2,1,0:T(8,128)(2,1)} %image_hbm.1, bf16[3,3,192,384]{3,2,1,0:T(8,128)(2,1)} %conv_hbm.1, bf16[384,1152]{1,0:T(8,128)(2,1)} %qkv_hbm.1, bf16[384,384]{1,0:T(8,128)(2,1)} %proj_hbm.1, f32[384]{0:T(512)} %conv_bias_hbm.1, f32[384]{0:T(512)} %merge_gain_hbm.1, f32[384]{0:T(512)} %merge_shift_hbm.1, ...), custom_call_target="tpu_custom_call" | custom-call | tf_op jit(solution)/shard_map/pallas_call | solution.py:254
  38.8 1.6 %copy.12 = bf16[16,16,384]{2,1,0:T(8,128)(2,1)} copy(bf16[16,16,384]{2,1,0:T(8,128)(2,1)} %shard_map.100) | data formatting | bytes 393216

commit v3 on v1

v3 whole, which is shorter than its diff:
```python
import math

import jax
import jax.numpy as jnp
from jax import lax
from jax.experimental import pallas as pl
from jax.experimental.pallas import tpu as pltpu
from jax.sharding import PartitionSpec as P

HEADS = 16
PEERS = 16
DEPTH = 24
HALF = 192
DIM = 384
TOKENS = 256
CHUNK = 512
F32 = jnp.float32
BF16 = jnp.bfloat16
MESH = pl.DeviceIdType.MESH
FAR_FIRST = (2, 1, 3, 0)


def layer_norm(values, gain, shift):
    center = values - jnp.mean(values, -1, keepdims=True)
    spread = jnp.mean(center * center, -1, keepdims=True)
    return center * lax.rsqrt(spread + 1e-05) * gain + shift


def by_stripe(values):
    pieces = [values[16 * i + 8 * s : 16 * i + 8 * s + 8] for s in range(2) for i in range(16)]
    return jnp.concatenate(pieces, 0)


def by_row(values):
    pieces = [values[128 * s + 8 * i : 128 * s + 8 * i + 8] for i in range(16) for s in range(2)]
    return jnp.concatenate(pieces, 0)


def lanes_in(refs, rows):
    return jnp.concatenate([ref[rows, :] for ref in refs], 1)


def kernel(
    image_hbm, conv_hbm, qkv_hbm, proj_hbm,
    conv_bias_hbm, merge_gain_hbm, merge_shift_hbm, norm_gain_hbm, norm_shift_hbm, proj_bias_hbm,
    out_ref,
    conv_bias, merge_gain, merge_shift, norm_gain, norm_shift, proj_bias,
    image, conv_w, qkv_w, proj_w, padded, phases, qkv_t,
    edge_low, edge_high,
    column, halo_row, halo_col, halo_corner,
    merged_0, merged_1, merged_2, tokens_0, tokens_1, tokens_2, normed_0, normed_1, normed_2,
    send_kv, recv_kv, send_q, recv_q, back_send, back_recv,
    keys, value_t, scores,
    load_sem, halo_send, halo_recv,
    kv_send_sem, kv_recv_sem, q_send_sem, q_recv_sem, back_send_sem, back_recv_sem,
):
    me_r = lax.axis_index("row")
    me_c = lax.axis_index("col")
    me = (me_c, me_r)
    down, up = lax.rem(me_r + 1, PEERS), lax.rem(me_r + PEERS - 1, PEERS)
    right, left = lax.rem(me_c + 1, PEERS), lax.rem(me_c + PEERS - 1, PEERS)
    merged_refs = (merged_0, merged_1, merged_2)
    token_refs = (tokens_0, tokens_1, tokens_2)
    normed_refs = (normed_0, normed_1, normed_2)

    def device(axis, peer):
        return (me_r, peer) if axis == 0 else (peer, me_c)

    loads = [
        pltpu.make_async_copy(source, target, load_sem.at[place])
        for place, (source, target) in enumerate([
            (image_hbm, image), (qkv_hbm, qkv_w), (conv_hbm, conv_w), (conv_bias_hbm, conv_bias),
            (merge_gain_hbm, merge_gain), (merge_shift_hbm, merge_shift), (norm_gain_hbm, norm_gain),
            (norm_shift_hbm, norm_shift), (proj_bias_hbm, proj_bias), (proj_hbm, proj_w)])
    ]
    for load in loads:
        load.start()

    peers = ([], [])
    for axis in range(2):
        block, place = me[axis] // 4, lax.rem(me[axis], 4)
        for outer in FAR_FIRST:
            for inner in FAR_FIRST:
                if outer or inner:
                    if axis == 0:
                        peers[0].append(lax.rem(block + outer, 4) * 4 + lax.rem(place + inner, 4))
                    else:
                        peers[1].append(lax.rem(block + inner, 4) * 4 + lax.rem(place + outer, 4))

    barrier = pltpu.get_barrier_semaphore()
    for step in range(PEERS - 1):
        for axis in (1, 0):
            pl.semaphore_signal(barrier, inc=1, device_id=device(axis, peers[axis][step]), device_id_type=MESH)
    pl.semaphore_signal(barrier, inc=1, device_id=(down, right), device_id_type=MESH)
    pl.semaphore_signal(barrier, inc=1, device_id=(up, left), device_id_type=MESH)

    def pad(rows, cols, values):
        padded[0, rows, cols, :] = values[:, :, 0:128]
        padded[1, rows, cols, 0:64] = values[:, :, 128:192]

    pad(slice(0, 1), slice(0, 40), jnp.zeros((1, 40, 192), F32))
    pad(slice(1, 33), slice(0, 8), jnp.zeros((32, 8, 192), F32))
    value_t[0, 24:32, :] = jnp.ones((8, 2048), BF16)
    value_t[1, 24:32, :] = jnp.ones((8, 2048), BF16)
    loads[0].wait()
    pad(slice(1, 33), slice(8, 40), image[...].astype(F32))
    column[:, 0:128] = padded[0, 1:33, 39:40, :].reshape(32, 128).astype(BF16)
    column[:, 128:192] = padded[1, 1:33, 39:40, 0:64].reshape(32, 64).astype(BF16)
    loads[1].wait()
    qkv_t[...] = qkv_w[...].T

    pl.semaphore_wait(barrier, 2 * (PEERS - 1) + 2)
    halos = [
        pltpu.make_async_remote_copy(
            src_ref=image.at[31], dst_ref=halo_row, send_sem=halo_send.at[0], recv_sem=halo_recv.at[0],
            device_id=(down, me_c), device_id_type=MESH),
        pltpu.make_async_remote_copy(
            src_ref=column, dst_ref=halo_col, send_sem=halo_send.at[1], recv_sem=halo_recv.at[1],
            device_id=(me_r, right), device_id_type=MESH),
        pltpu.make_async_remote_copy(
            src_ref=column.at[pl.ds(16, 16)], dst_ref=halo_corner, send_sem=halo_send.at[2], recv_sem=halo_recv.at[2],
            device_id=(down, right), device_id_type=MESH),
    ]
    for halo in halos:
        halo.start()

    for load in loads[2:]:
        load.wait()
    for tap in range(3):
        low = padded[0, :, pl.ds(7 + tap, 16, stride=2), :].astype(BF16)
        high = padded[1, :, pl.ds(7 + tap, 16, stride=2), :].astype(BF16)
        phases[tap, :, :, :, 0:128] = low.reshape(17, 2, 16, 128)
        phases[tap, :, :, :, 128:192] = high[:, :, 0:64].reshape(17, 2, 16, 64)
    merged = jnp.zeros((TOKENS, DIM), F32)
    for a in range(3):
        for b in range(3):
            window = phases[b, pl.ds(a // 2, 16), a % 2].reshape(TOKENS, 192)
            merged = merged + jnp.dot(window, conv_w[a, b], preferred_element_type=F32)

    def norms(values):
        merge_affine = merge_gain[...][None, :], merge_shift[...][None, :]
        tokens = layer_norm(values + conv_bias[...][None, :], *merge_affine).astype(BF16).astype(F32)
        return tokens, layer_norm(tokens, norm_gain[...][None, :], norm_shift[...][None, :])

    def keep(refs, rows, values):
        for place, ref in enumerate(refs):
            ref[rows, :] = values[:, 128 * place : 128 * place + 128]

    tokens, normed = norms(merged)
    keep(merged_refs, slice(None), merged)
    keep(token_refs, slice(None), tokens)
    keep(normed_refs, slice(None), normed)

    for halo in halos:
        halo.wait()
    has_up, has_left = me_r > 0, me_c > 0
    corner = jnp.where(jnp.logical_and(has_up, has_left), halo_corner[...].astype(F32)[15:16], 0.0)
    edge_row = jnp.where(has_up, halo_row[...].astype(F32), 0.0)
    edge_col = jnp.where(has_left, halo_col[...].astype(F32), 0.0)

    def edge_store(rows, values):
        edge_low[rows, :] = values[:, 0:128]
        edge_high[rows, 0:64] = values[:, 128:192]

    def edge_load(start):
        rows = pl.ds(start, 16, stride=2)
        return jnp.concatenate([edge_low[rows, :], edge_high[rows, :][:, 0:64]], 1).astype(BF16)

    edge_store(slice(7, 8), corner)
    edge_store(slice(8, 40), edge_row)
    edge_store(slice(47, 48), jnp.zeros((1, 192), F32))
    edge_store(slice(48, 80), edge_col)
    rows_in = [edge_load(7 + b) for b in range(3)]
    cols_in = [edge_load(47 + a) for a in range(3)]
    shared = jnp.dot(jnp.concatenate([rows_in[0], cols_in[0]], 0), conv_w[0, 0], preferred_element_type=F32)
    row_fix, col_fix = shared[0:16], shared[16:32]
    for tap in (1, 2):
        row_fix = row_fix + jnp.dot(rows_in[tap], conv_w[0, tap], preferred_element_type=F32)
        col_fix = col_fix + jnp.dot(cols_in[tap], conv_w[tap, 0], preferred_element_type=F32)
    first = lax.broadcasted_iota(jnp.int32, (16, DIM), 0) == 0
    row_fix = row_fix + jnp.where(first, col_fix[0:1], 0.0)
    upper, side = slice(0, 16), pl.ds(0, 16, stride=16)
    fixed = jnp.concatenate(
        [lanes_in(merged_refs, upper) + row_fix, lanes_in(merged_refs, side) + col_fix], 0)
    tokens, normed = norms(fixed)
    for refs, values in ((token_refs, tokens), (normed_refs, normed)):
        keep(refs, side, values[16:32])
        keep(refs, upper, values[0:16])
    normed = lanes_in(normed_refs, slice(None))

    def project(values, base, part):
        rows = slice(part * DIM + base, part * DIM + base + HALF)
        return lax.dot_general(qkv_t[rows, :], values, (((1,), (1,)), ((), ())), preferred_element_type=F32)

    def leave(axis, send, recv, sends, recvs, peer):
        return pltpu.make_async_remote_copy(
            src_ref=send.at[axis, peer], dst_ref=recv.at[axis, me[axis]],
            send_sem=sends.at[axis], recv_sem=recvs.at[axis],
            device_id=device(axis, peer), device_id_type=MESH)

    def all_of(axis, send, recv, sends, recvs):
        most = pl.ds(0, PEERS - 1)
        return pltpu.make_async_remote_copy(
            src_ref=send.at[axis, most], dst_ref=recv.at[axis, most],
            send_sem=sends.at[axis], recv_sem=recvs.at[axis],
            device_id=device(axis, peers[axis][0]), device_id_type=MESH)

    kv = (send_kv, recv_kv, kv_send_sem, kv_recv_sem)
    queries = (send_q, recv_q, q_send_sem, q_recv_sem)
    back = (back_send, back_recv, back_send_sem, back_recv_sem)

    for axis in range(2):
        values = (normed if axis == 0 else by_stripe(normed)).astype(BF16)
        key_part, value_part = (project(values, axis * HALF, part) for part in (1, 2))
        for head in range(HEADS // 2):
            rows = slice(DEPTH * head, DEPTH * head + DEPTH)
            block = jnp.concatenate([key_part[rows], value_part[rows]], 0).astype(BF16)
            send_kv[axis, head] = block[:, :128]
            send_kv[axis, 8 + head] = block[:, 128:]
        for peer in peers[axis]:
            leave(axis, *kv, peer).start()
        query_part = project(values, axis * HALF, 0)
        for head in range(HEADS // 2):
            block = query_part[DEPTH * head : DEPTH * head + DEPTH].astype(BF16)
            send_q[axis, head] = block[:, :128]
            send_q[axis, 8 + head] = block[:, 128:]
        for peer in peers[axis] if axis == 0 else []:
            leave(axis, *queries, peer).start()
    for axis in range(2):
        recv_kv[axis, me[axis]] = send_kv[axis, me[axis]]
        recv_q[axis, me[axis]] = send_q[axis, me[axis]]

    def take_keys(axis):
        all_of(axis, *kv).wait_recv()
        for peer in range(PEERS):
            rows = slice(128 * peer, 128 * peer + 128)
            block = recv_kv[axis, peer]
            value_t[axis, 0:24, rows] = block[24:48]
            own = jnp.concatenate([block.astype(F32)[0:24], jnp.zeros((104, 128), F32)], 0)
            keys[axis, rows, :] = own.T.astype(BF16)

    def take_queries(axis, place):
        pair = [2 * place, 2 * place + 1]
        return jnp.concatenate([recv_q[axis, peer] for peer in pair], 1)

    def score(axis, query, buffer, chunk, highest):
        rows = slice(CHUNK * chunk, CHUNK * chunk + CHUNK)
        part = jnp.dot(keys[axis, rows, 0:24], query, preferred_element_type=F32)
        scores[buffer, rows, :] = part
        return jnp.maximum(highest, jnp.max(part.reshape(CHUNK // 8, 8, 256), 0))

    def gather(axis, buffer, chunk, highest, summed):
        rows = slice(CHUNK * chunk, CHUNK * chunk + CHUNK)
        weights = jnp.exp2((scores[buffer, rows, :] - highest) * (math.log2(math.e) / math.sqrt(DEPTH)))
        return summed + jnp.dot(value_t[axis, :, rows], weights.astype(BF16), preferred_element_type=F32)

    def finish(axis, place, own, summed):
        result = (summed[0:24] / summed[24:25]).astype(BF16)
        back_send[axis, 2 * place] = result[:, :128]
        back_send[axis, 2 * place + 1] = result[:, 128:]
        for peer in [2 * place + 1 - lax.rem(me[axis], 2)] if own else [2 * place, 2 * place + 1]:
            leave(axis, *back, peer).start()

    def place_of(axis, tile):
        outer, inner = me[axis] // 4, lax.rem(me[axis], 4) // 2
        return lax.rem(outer + 1 + tile, 4) * 2 + lax.rem(inner + 1 + tile // 4, 2)

    def step(ahead, behind, buffer, highest):
        later = jnp.full((8, 256), -jnp.inf, F32)
        summed = jnp.zeros((32, 256), F32)
        if ahead is not None:
            query = take_queries(ahead[0], place_of(*ahead))
        for chunk in range(2048 // CHUNK):
            if ahead is not None:
                later = score(ahead[0], query, buffer, chunk, later)
            if behind is not None:
                summed = gather(behind[0], 1 - buffer, chunk, highest, summed)
        if behind is not None:
            finish(behind[0], place_of(*behind), isinstance(behind[1], int) and behind[1] == 7, summed)
        return jnp.max(later, 0, keepdims=True)

    def steps(axis, highest):
        def two(trip, highest):
            highest = step((axis, 2 * trip + 1), (axis, 2 * trip), 1, highest)
            return step((axis, 2 * trip + 2), (axis, 2 * trip + 1), 0, highest)

        highest = lax.fori_loop(0, 3, two, highest)
        return step((axis, 7), (axis, 6), 1, highest)

    take_keys(0)
    all_of(0, *queries).wait_recv()
    highest = step((0, 0), None, 0, None)
    for peer in peers[1]:
        leave(1, *queries, peer).start()
    highest = steps(0, highest)
    take_keys(1)
    all_of(1, *queries).wait_recv()
    highest = step((1, 0), (0, 7), 0, highest)
    highest = steps(1, highest)
    step(None, (1, 7), 0, highest)
    for axis in range(2):
        back_recv[axis, me[axis]] = back_send[axis, me[axis]]

    def mix(axis):
        outs = []
        for stripe in range(2):
            heads = [back_recv[axis, 8 * stripe + head].astype(F32) for head in range(8)]
            mixed = jnp.concatenate(heads, 0).T.astype(BF16)
            outs.append(jnp.dot(mixed, proj_w[axis * HALF : axis * HALF + HALF, :], preferred_element_type=F32))
        return jnp.concatenate(outs, 0)

    for axis in range(2):
        all_of(axis, *kv).wait_send()
        all_of(axis, *queries).wait_send()
    all_of(0, *back).wait_send()
    all_of(0, *back).wait_recv()
    total = mix(0) + lanes_in(token_refs, slice(None)) + proj_bias[...][None, :]
    all_of(1, *back).wait_send()
    all_of(1, *back).wait_recv()
    out_ref[...] = (total + by_row(mix(1))).astype(BF16).reshape(16, 16, DIM)


def on_device(image, conv_weight, conv_bias, merge_gain, merge_shift, norm_gain, norm_shift, qkv_weight, proj_weight, proj_bias):
    dma = pltpu.SemaphoreType.DMA
    return pl.pallas_call(
        kernel,
        out_shape=pltpu.VMEM((16, 16, DIM), BF16),
        in_specs=[pl.BlockSpec(memory_space=pltpu.HBM)] * 10,
        out_specs=pl.BlockSpec(memory_space=pltpu.VMEM),
        scratch_shapes=[pltpu.VMEM((DIM,), F32)] * 6
        + [
            pltpu.VMEM((32, 32, 192), BF16),
            pltpu.VMEM((3, 3, 192, DIM), BF16),
            pltpu.VMEM((DIM, 3 * DIM), BF16),
            pltpu.VMEM((DIM, DIM), BF16),
            pltpu.VMEM((2, 34, 40, 128), F32),
            pltpu.VMEM((3, 17, 2, 16, 192), BF16),
            pltpu.VMEM((3 * DIM, DIM), BF16),
            pltpu.VMEM((80, 128), F32),
            pltpu.VMEM((80, 128), F32),
            pltpu.VMEM((32, 192), BF16),
            pltpu.VMEM((32, 192), BF16),
            pltpu.VMEM((32, 192), BF16),
            pltpu.VMEM((16, 192), BF16),
        ]
        + [pltpu.VMEM((TOKENS, 128), F32)] * 9
        + [pltpu.VMEM((2, PEERS, 2 * DEPTH, 128), BF16)] * 2
        + [pltpu.VMEM((2, PEERS, DEPTH, 128), BF16)] * 4
        + [
            pltpu.VMEM((2, 2048, 128), BF16),
            pltpu.VMEM((2, 32, 2048), BF16),
            pltpu.VMEM((2, 2048, 256), F32),
            dma((10,)),
            dma((3,)),
            dma((3,)),
        ]
        + [dma((2,))] * 6,
        compiler_params=pltpu.CompilerParams(
            collective_id=0, has_side_effects=True, vmem_limit_bytes=66000000),
    )(image, conv_weight, qkv_weight, proj_weight, conv_bias, merge_gain, merge_shift, norm_gain, norm_shift, proj_bias)


def solution(mesh):
    return jax.shard_map(
        on_device,
        mesh=mesh,
        in_specs=(P("row", "col", None), P(), P(), P(), P(), P(), P(), P(), P(), P()),
        out_specs=P("row", "col", None),
        check_vma=False,
    )
```

time: 55 us -> 37.7 us (0.69)
  local copies, waits for them, and re-layouts: 9.26 us -> 0.68 us
  Pallas kernels: 45.3 us -> 37 us
    unnamed x21 -> x1, local copies, waits for them, and re-layouts: 9.26 us -> 0.68 us
    pallas_call x1, Pallas kernels: 45.3 us -> 37 us  [on_device(): pl.pallas_call(kernel, out_shape=pltpu.VMEM((16, 16, DIM), BF16), in_spec...]
where the time goes in v3:
time: 37.7 us; the launch traced here: 37.6 us
  Pallas kernels  37 us (98%)
  local copies, waits for them, and re-layouts  0.68 us (2%)
    pallas_call x1, Pallas kernels, on_device(): pl.pallas_call(kernel, out_shape=pltpu.VMEM((16, 16, DIM), BF16), in_spec...  37 us

profile of v3, /device:TPU:32, one launch (start us, length us, event | category | flops | bytes accessed | tf_op | source)
XLA Modules:
  0.0 37.6 jit_solution(16447450771494469275)
XLA Ops:
  0.0 37.0 %shard_map.100 = bf16[16,16,384]{2,1,0:T(8,128)(2,1)S(1)} custom-call(bf16[32,32,192]{2,1,0:T(8,128)(2,1)} %image_hbm.1, bf16[3,3,192,384]{3,2,1,0:T(8,128)(2,1)} %conv_hbm.1, bf16[384,1152]{1,0:T(8,128)(2,1)} %qkv_hbm.1, bf16[384,384]{1,0:T(8,128)(2,1)} %proj_hbm.1, f32[384]{0:T(512)} %conv_bias_hbm.1, f32[384]{0:T(512)} %merge_gain_hbm.1, ...), custom_call_target="tpu_custom_call" | custom-call | tf_op jit(solution)/shard_map/pallas_call | solution.py:325
  37.0 0.7 %copy.12 = bf16[16,16,384]{2,1,0:T(8,128)(2,1)} copy(bf16[16,16,384]{2,1,0:T(8,128)(2,1)S(1)} %shard_map.100) | data formatting | bytes 393216

commit v4 on v3

--- a/solution.py
+++ b/solution.py
@@ -52,7 +52,7 @@
     send_kv, recv_kv, send_q, recv_q, back_send, back_recv,
     keys, value_t, scores,
     load_sem, halo_send, halo_recv,
-    kv_send_sem, kv_recv_sem, q_send_sem, q_recv_sem, back_send_sem, back_recv_sem,
+    kv_send_sem, kv_recv_sem, q_send_sem, q_recv_sem, back_send_sem, back_recv_sem, pair_sem,
 ):
     me_r = lax.axis_index("row")
     me_c = lax.axis_index("col")
@@ -151,12 +151,8 @@
     keep(token_refs, slice(None), tokens)
     keep(normed_refs, slice(None), normed)
 
-    for halo in halos:
-        halo.wait()
     has_up, has_left = me_r > 0, me_c > 0
-    corner = jnp.where(jnp.logical_and(has_up, has_left), halo_corner[...].astype(F32)[15:16], 0.0)
-    edge_row = jnp.where(has_up, halo_row[...].astype(F32), 0.0)
-    edge_col = jnp.where(has_left, halo_col[...].astype(F32), 0.0)
+    upper, side = slice(0, 16), pl.ds(0, 16, stride=16)
 
     def edge_store(rows, values):
         edge_low[rows, :] = values[:, 0:128]
@@ -166,27 +162,44 @@
         rows = pl.ds(start, 16, stride=2)
         return jnp.concatenate([edge_low[rows, :], edge_high[rows, :][:, 0:64]], 1).astype(BF16)
 
-    edge_store(slice(7, 8), corner)
-    edge_store(slice(8, 40), edge_row)
-    edge_store(slice(47, 48), jnp.zeros((1, 192), F32))
-    edge_store(slice(48, 80), edge_col)
-    rows_in = [edge_load(7 + b) for b in range(3)]
-    cols_in = [edge_load(47 + a) for a in range(3)]
-    shared = jnp.dot(jnp.concatenate([rows_in[0], cols_in[0]], 0), conv_w[0, 0], preferred_element_type=F32)
-    row_fix, col_fix = shared[0:16], shared[16:32]
-    for tap in (1, 2):
-        row_fix = row_fix + jnp.dot(rows_in[tap], conv_w[0, tap], preferred_element_type=F32)
-        col_fix = col_fix + jnp.dot(cols_in[tap], conv_w[tap, 0], preferred_element_type=F32)
-    first = lax.broadcasted_iota(jnp.int32, (16, DIM), 0) == 0
-    row_fix = row_fix + jnp.where(first, col_fix[0:1], 0.0)
-    upper, side = slice(0, 16), pl.ds(0, 16, stride=16)
-    fixed = jnp.concatenate(
-        [lanes_in(merged_refs, upper) + row_fix, lanes_in(merged_refs, side) + col_fix], 0)
-    tokens, normed = norms(fixed)
-    for refs, values in ((token_refs, tokens), (normed_refs, normed)):
-        keep(refs, side, values[16:32])
-        keep(refs, upper, values[0:16])
-    normed = lanes_in(normed_refs, slice(None))
+    def left_edge():
+        halos[1].wait()
+        edge_store(slice(47, 48), jnp.zeros((1, 192), F32))
+        edge_store(slice(48, 80), jnp.where(has_left, halo_col[...].astype(F32), 0.0))
+        fix = jnp.zeros((16, DIM), F32)
+        for tap in range(3):
+            fix = fix + jnp.dot(edge_load(47 + tap), conv_w[tap, 0], preferred_element_type=F32)
+        fixed = lanes_in(merged_refs, side) + fix
+        keep(merged_refs, side, fixed)
+        tokens, normed = norms(fixed)
+        keep(token_refs, side, tokens)
+        keep(normed_refs, side, normed)
+
+    def upper_edge():
+        halos[0].wait()
+        halos[2].wait()
+        corner = jnp.where(jnp.logical_and(has_up, has_left), halo_corner[...].astype(F32)[15:16], 0.0)
+        edge_store(slice(7, 8), corner)
+        edge_store(slice(8, 40), jnp.where(has_up, halo_row[...].astype(F32), 0.0))
+        fixed = lanes_in(merged_refs, upper)
+        for tap in range(3):
+            fixed = fixed + jnp.dot(edge_load(7 + tap), conv_w[0, tap], preferred_element_type=F32)
+        tokens, normed = norms(fixed)
+        keep(token_refs, upper, tokens)
+        keep(normed_refs, upper, normed)
+
+    def leave_query(peer):
+        return pltpu.make_async_remote_copy(
+            src_ref=send_q.at[0, peer], dst_ref=recv_q.at[0, me_c],
+            send_sem=q_send_sem.at[0], recv_sem=pair_sem.at[me_c // 2],
+            device_id=(me_r, peer), device_id_type=MESH)
+
+    def wait_queries(place, count):
+        several = pl.ds(0, count)
+        pltpu.make_async_remote_copy(
+            src_ref=send_q.at[0, several], dst_ref=recv_q.at[0, several],
+            send_sem=q_send_sem.at[0], recv_sem=pair_sem.at[place],
+            device_id=(me_r, peers[0][0]), device_id_type=MESH).wait_recv()
 
     def project(values, base, part):
         rows = slice(part * DIM + base, part * DIM + base + HALF)
@@ -209,29 +222,50 @@
     queries = (send_q, recv_q, q_send_sem, q_recv_sem)
     back = (back_send, back_recv, back_send_sem, back_recv_sem)
 
-    for axis in range(2):
-        values = (normed if axis == 0 else by_stripe(normed)).astype(BF16)
-        key_part, value_part = (project(values, axis * HALF, part) for part in (1, 2))
+    def to_stripe(stripe, copy_to):
+        for head in range(HEADS // 2):
+            peer = 8 * stripe + lax.rem(me_c + 4 + head, 8)
+
+            @pl.when(peer != me_c)
+            def _():
+                copy_to(peer).start()
+
+    for stripe in (1, 0):
+        if stripe:
+            left_edge()
+        else:
+            upper_edge()
+        values = lanes_in(normed_refs, slice(128 * stripe, 128 * stripe + 128)).astype(BF16)
+        key_part, value_part = (project(values, 0, part) for part in (1, 2))
         for head in range(HEADS // 2):
             rows = slice(DEPTH * head, DEPTH * head + DEPTH)
             block = jnp.concatenate([key_part[rows], value_part[rows]], 0).astype(BF16)
-            send_kv[axis, head] = block[:, :128]
-            send_kv[axis, 8 + head] = block[:, 128:]
-        for peer in peers[axis]:
-            leave(axis, *kv, peer).start()
-        query_part = project(values, axis * HALF, 0)
+            send_kv[0, 8 * stripe + head] = block
+        to_stripe(stripe, lambda peer: leave(0, *kv, peer))
+        query_part = project(values, 0, 0)
         for head in range(HEADS // 2):
-            block = query_part[DEPTH * head : DEPTH * head + DEPTH].astype(BF16)
-            send_q[axis, head] = block[:, :128]
-            send_q[axis, 8 + head] = block[:, 128:]
-        for peer in peers[axis] if axis == 0 else []:
-            leave(axis, *queries, peer).start()
+            send_q[0, 8 * stripe + head] = query_part[DEPTH * head : DEPTH * head + DEPTH].astype(BF16)
+        to_stripe(stripe, leave_query)
+
+    values = by_stripe(lanes_in(normed_refs, slice(None))).astype(BF16)
+    key_part, value_part = (project(values, HALF, part) for part in (1, 2))
+    for head in range(HEADS // 2):
+        rows = slice(DEPTH * head, DEPTH * head + DEPTH)
+        block = jnp.concatenate([key_part[rows], value_part[rows]], 0).astype(BF16)
+        send_kv[1, head] = block[:, :128]
+        send_kv[1, 8 + head] = block[:, 128:]
+    for peer in peers[1]:
+        leave(1, *kv, peer).start()
+    query_part = project(values, HALF, 0)
+    for head in range(HEADS // 2):
+        block = query_part[DEPTH * head : DEPTH * head + DEPTH].astype(BF16)
+        send_q[1, head] = block[:, :128]
+        send_q[1, 8 + head] = block[:, 128:]
     for axis in range(2):
         recv_kv[axis, me[axis]] = send_kv[axis, me[axis]]
         recv_q[axis, me[axis]] = send_q[axis, me[axis]]
 
     def take_keys(axis):
-        all_of(axis, *kv).wait_recv()
         for peer in range(PEERS):
             rows = slice(128 * peer, 128 * peer + 128)
             block = recv_kv[axis, peer]
@@ -263,12 +297,17 @@
 
     def place_of(axis, tile):
         outer, inner = me[axis] // 4, lax.rem(me[axis], 4) // 2
-        return lax.rem(outer + 1 + tile, 4) * 2 + lax.rem(inner + 1 + tile // 4, 2)
+        return lax.rem(outer + axis + tile, 4) * 2 + lax.rem(inner + axis + tile // 4, 2)
+
+    def is_own(axis, tile):
+        return isinstance(tile, int) and tile == 7 * axis
 
     def step(ahead, behind, buffer, highest):
         later = jnp.full((8, 256), -jnp.inf, F32)
         summed = jnp.zeros((32, 256), F32)
         if ahead is not None:
+            if ahead[0] == 0:
+                wait_queries(place_of(*ahead), 1 if is_own(*ahead) else 2)
             query = take_queries(ahead[0], place_of(*ahead))
         for chunk in range(2048 // CHUNK):
             if ahead is not None:
@@ -276,27 +315,30 @@
             if behind is not None:
                 summed = gather(behind[0], 1 - buffer, chunk, highest, summed)
         if behind is not None:
-            finish(behind[0], place_of(*behind), isinstance(behind[1], int) and behind[1] == 7, summed)
+            finish(behind[0], place_of(*behind), is_own(*behind), summed)
         return jnp.max(later, 0, keepdims=True)
 
-    def steps(axis, highest):
+    def steps(axis, initial, highest):
         def two(trip, highest):
-            highest = step((axis, 2 * trip + 1), (axis, 2 * trip), 1, highest)
-            return step((axis, 2 * trip + 2), (axis, 2 * trip + 1), 0, highest)
-
-        highest = lax.fori_loop(0, 3, two, highest)
-        return step((axis, 7), (axis, 6), 1, highest)
-
-    take_keys(0)
-    all_of(0, *queries).wait_recv()
-    highest = step((0, 0), None, 0, None)
+            tile = initial + 2 * trip
+            highest = step((axis, tile), (axis, tile - 1), initial % 2, highest)
+            return step((axis, tile + 1), (axis, tile), 1 - initial % 2, highest)
+
+        return lax.fori_loop(0, 3, two, highest)
+
+    all_of(0, *kv).wait_recv()
     for peer in peers[1]:
         leave(1, *queries, peer).start()
-    highest = steps(0, highest)
+    take_keys(0)
+    highest = step((0, 0), None, 0, None)
+    highest = step((0, 1), (0, 0), 1, highest)
+    highest = steps(0, 2, highest)
+    all_of(1, *kv).wait_recv()
     take_keys(1)
     all_of(1, *queries).wait_recv()
     highest = step((1, 0), (0, 7), 0, highest)
-    highest = steps(1, highest)
+    highest = steps(1, 1, highest)
+    highest = step((1, 7), (1, 6), 1, highest)
     step(None, (1, 7), 0, highest)
     for axis in range(2):
         back_recv[axis, me[axis]] = back_send[axis, me[axis]]
@@ -354,7 +396,8 @@
             dma((3,)),
             dma((3,)),
         ]
-        + [dma((2,))] * 6,
+        + [dma((2,))] * 6
+        + [dma((PEERS // 2,))],
         compiler_params=pltpu.CompilerParams(
             collective_id=0, has_side_effects=True, vmem_limit_bytes=66000000),
     )(image, conv_weight, qkv_weight, proj_weight, conv_bias, merge_gain, merge_shift, norm_gain, norm_shift, proj_bias)

time: 37.7 us -> 36.1 us (0.958); the launches traced: 37.6 us -> 35.5 us
  Pallas kernels: 37 us -> 34.8 us
    pallas_call x1, Pallas kernels: 37 us -> 34.8 us  [on_device(): pl.pallas_call(kernel, out_shape=pltpu.VMEM((16, 16, DIM), BF16), in_spec...]
where the time goes in v4:
time: 36.1 us; the launch traced here: 35.5 us
  Pallas kernels  34.8 us (96%)
  local copies, waits for them, and re-layouts  0.68 us (2%)
    pallas_call x1, Pallas kernels, on_device(): pl.pallas_call(kernel, out_shape=pltpu.VMEM((16, 16, DIM), BF16), in_spec...  34.8 us

profile of v4, /device:TPU:32, one launch (start us, length us, event | category | flops | bytes accessed | tf_op | source)
XLA Modules:
  0.0 35.5 jit_solution(12842739124365776597)
XLA Ops:
  0.0 34.8 %shard_map.100 = bf16[16,16,384]{2,1,0:T(8,128)(2,1)S(1)} custom-call(bf16[32,32,192]{2,1,0:T(8,128)(2,1)} %image_hbm.1, bf16[3,3,192,384]{3,2,1,0:T(8,128)(2,1)} %conv_hbm.1, bf16[384,1152]{1,0:T(8,128)(2,1)} %qkv_hbm.1, bf16[384,384]{1,0:T(8,128)(2,1)} %proj_hbm.1, f32[384]{0:T(512)} %conv_bias_hbm.1, f32[384]{0:T(512)} %merge_gain_hbm.1, ...), custom_call_target="tpu_custom_call" | custom-call | tf_op jit(solution)/shard_map/pallas_call | solution.py:367
  34.8 0.7 %copy.12 = bf16[16,16,384]{2,1,0:T(8,128)(2,1)} copy(bf16[16,16,384]{2,1,0:T(8,128)(2,1)S(1)} %shard_map.100) | data formatting | bytes 393216
